TPU v7x, 32 devices: a whole 2x2x4 slice. The times are simulated.
32 devices in a mesh: groups: 2 (over x), seq: 16 (over z, y, core).
Axes of the slice: x: 2, y: 2, z: 4, core: 2. Of those that a mesh axis runs over, the one named last changes fastest.
Arguments:
- clip_tokens: bfloat16 [32, 128, 512], P(('groups', 'seq')), parts along dimension 0, may hold values from -6 to 6
- spatial_qkv: bfloat16 [512, 1536], replicated, may hold values from -4.6403883 to 4.6403883
- spatial_out: bfloat16 [512, 512], replicated, may hold values from -0.5 to 0.5
- temporal_qkv: bfloat16 [512, 1536], replicated, may hold values from -4.6403883 to 4.6403883
- temporal_out: bfloat16 [512, 512], replicated, may hold values from -0.5 to 0.5
- mlp_up: bfloat16 [512, 2048], replicated, may hold values from -0.25 to 0.25
- mlp_down: bfloat16 [2048, 512], replicated, may hold values from -0.25 to 0.25
Outputs:
- layer_out: bfloat16 [32, 128, 512], P(('groups', 'seq')), parts along dimension 0
There are 2 independent parts, one for each index of `groups`. A program takes and returns all parts, laid end to end along the dimension named above; an argument that names none is the same for every part. Nothing has to cross between parts.
All inputs are finite; a program needn't handle non-finite values.
Results may differ from a plain program's by a relative error of at most 0.013.
Values may be sent and summed in bfloat16 or wider, within the bound.
A program may use at most 128 MiB of HBM per device.

v0:
```python
import jax
import jax.numpy as jnp
from jax import lax
from jax.sharding import PartitionSpec as P

HEADS = 8


def norm_rows(values):
    center = values - jnp.mean(values, axis=-1, keepdims=True)
    spread = jnp.mean(center * center, axis=-1, keepdims=True)
    return (center * lax.rsqrt(spread + 1e-05)).astype(jnp.bfloat16)


def softmax_rows(scores):
    row_max = jnp.max(scores, axis=-1, keepdims=True)
    raised = jnp.exp(scores - row_max)
    return (raised / jnp.sum(raised, axis=-1, keepdims=True)).astype(jnp.bfloat16)


def spatial_frame(frame_rows, w_qkv, w_out):
    patches, model_width = frame_rows.shape
    head_width = model_width // HEADS
    packed = jnp.dot(
        norm_rows(frame_rows.astype(jnp.float32)), w_qkv, preferred_element_type=jnp.float32
    )
    packed = packed.astype(jnp.bfloat16).reshape(patches, 3, HEADS, head_width)
    key_rows = packed[:, 1]
    value_rows = packed[:, 2]
    block_rows = min(512, patches)
    query_rows = packed[:, 0].reshape(patches // block_rows, block_rows, HEADS, head_width)

    def one_block(query_block):
        scores = jnp.einsum(
            "qhd,khd->hqk", query_block, key_rows, preferred_element_type=jnp.float32
        ) * head_width ** (-0.5)
        weights = softmax_rows(scores)
        attended = jnp.einsum(
            "hqk,khd->qhd", weights, value_rows, preferred_element_type=jnp.float32
        )
        return attended.astype(jnp.bfloat16).reshape(block_rows, model_width)

    attended = lax.map(one_block, query_rows).reshape(patches, model_width)
    merged = frame_rows.astype(jnp.float32) + jnp.dot(
        attended, w_out, preferred_element_type=jnp.float32
    )
    return merged.astype(jnp.bfloat16)


def temporal_block(tokens, w_qkv, w_out):
    frames, count_rows, model_width = tokens.shape
    head_width = model_width // HEADS
    flat_rows = tokens.reshape(frames * count_rows, model_width)
    packed = jnp.dot(
        norm_rows(flat_rows.astype(jnp.float32)), w_qkv, preferred_element_type=jnp.float32
    )
    packed = packed.astype(jnp.bfloat16).reshape(frames, count_rows, 3, HEADS, head_width)
    scores = jnp.einsum(
        "fkhd,gkhd->khfg", packed[:, :, 0], packed[:, :, 1], preferred_element_type=jnp.float32
    ) * head_width ** (-0.5)
    weights = softmax_rows(scores)
    attended = jnp.einsum(
        "khfg,gkhd->fkhd", weights, packed[:, :, 2], preferred_element_type=jnp.float32
    )
    attended = attended.astype(jnp.bfloat16).reshape(frames * count_rows, model_width)
    merged = flat_rows.astype(jnp.float32) + jnp.dot(
        attended, w_out, preferred_element_type=jnp.float32
    )
    return merged.astype(jnp.bfloat16)


def feed_forward(tokens, w_up, w_down):
    raised = jnp.dot(
        norm_rows(tokens.astype(jnp.float32)), w_up, preferred_element_type=jnp.float32
    )
    hidden = jax.nn.gelu(raised, approximate=True).astype(jnp.bfloat16)
    merged = tokens.astype(jnp.float32) + jnp.dot(
        hidden, w_down, preferred_element_type=jnp.float32
    )
    return merged.astype(jnp.bfloat16)


def local(clip_tokens, spatial_qkv, spatial_out, temporal_qkv, temporal_out, mlp_up, mlp_down):
    frame_count, patches, model_width = clip_tokens.shape
    devices = lax.axis_size("seq")
    mixed = lax.map(
        lambda frame_rows: spatial_frame(frame_rows, spatial_qkv, spatial_out), clip_tokens
    )
    blocks = mixed.reshape(frame_count, devices, patches // devices, model_width)
    arrived = lax.all_to_all(blocks, "seq", split_axis=1, concat_axis=0, tiled=True)
    frames = arrived.shape[0]
    count_rows = arrived.shape[2]
    tokens = arrived.reshape(frames, count_rows, model_width)
    after_time = temporal_block(tokens, temporal_qkv, temporal_out)
    returned = after_time.reshape(frames, 1, count_rows, model_width)
    arrived_back = lax.all_to_all(returned, "seq", split_axis=0, concat_axis=1, tiled=True)
    result_rows = arrived_back.reshape(frame_count * patches, model_width)
    result_rows = feed_forward(result_rows, mlp_up, mlp_down)
    return result_rows.reshape(frame_count, patches, model_width)


def solution(mesh):
    in_specs = (P(("groups", "seq"), None, None), P(), P(), P(), P(), P(), P())
    out_specs = P(("groups", "seq"), None, None)
    return jax.shard_map(local, mesh=mesh, in_specs=in_specs, out_specs=out_specs, check_vma=False)
```

profile of v0, /device:TPU:0, one launch (start us, length us, event | category | flops | bytes accessed | tf_op | source)
XLA Modules:
  0.0 44.1 jit_solution(6778775718888962342)
XLA Ops:
  0.0 0.0 copy-start
  0.0 1.2 %convert_reduce_fusion.2 = f32[128]{0:T(128)S(1)} fusion(bf16[1,128,512]{2,1,0:T(8,128)(2,1)} %param.7), kind=kLoop, calls=%fused_computation.45 | loop fusion | flops 130944 | bytes 131584 | tf_op jit(solution)/shard_map/while/body/eval_jaxpr/reduce_sum | solution.py:10
  1.2 1.1 %fusion.31 = f32[128]{0:T(128)S(1)} fusion(bf16[1,128,512]{2,1,0:T(8,128)(2,1)} %param.7, f32[128]{0:T(128)S(1)} %broadcast_multiply_fusion.2), kind=kLoop, calls=%fused_computation.50 | loop fusion | flops 262016 | bytes 132096 | tf_op jit(solution)/shard_map/while/body/eval_jaxpr/reduce_sum | solution.py:11
  2.3 1.9 %convolution_convert_fusion.1 = bf16[128,1536]{1,0:T(8,128)(2,1)S(1)} fusion(bf16[512,1536]{1,0:T(8,128)(2,1)} %param.8, bf16[1,128,512]{2,1,0:T(8,128)(2,1)} %param.7, f32[128]{0:T(128)S(1)} %add_rsqrt_fusion.2, f32[128]{0:T(128)S(1)} %broadcast_multiply_fusion.2), kind=kOutput, calls=%fused_computation.3 | convolution fusion | flops 201785344 | bytes 2098176 | tf_op jit(solution)/shard_map/while/body/eval_jaxpr/dot_general | solution.py:24
  4.2 0.2 copy.23
  4.4 0.0 copy-start.1
  4.4 0.0 copy-start.2
  4.4 0.4 fusion.67
  4.8 1.1 %convolution_multiply_fusion = f32[8,128,128]{1,2,0:T(8,128)} fusion(bf16[128,3,8,64]{0,3,2,1:T(8,128)(2,1)S(1)} %bitcast.104), kind=kOutput, calls=%fused_computation.9 | convolution fusion | flops 16908288 | bytes 786432 | tf_op jit(solution)/shard_map/while/body/eval_jaxpr/while/body/eval_jaxpr/qhd,khd->hqk/dot_general | solution.py:34
  5.9 1.5 %convolution_convert_fusion.3 = bf16[8,64,128]{2,1,0:T(8,128)(2,1)S(1)} fusion(f32[8,128]{1,0:T(8,128)S(1)} %fusion.67, bf16[128,3,8,64]{0,3,2,1:T(8,128)(2,1)S(1)} %bitcast.105, f32[8,128,128]{1,2,0:T(8,128)} %convolution_multiply_fusion), kind=kOutput, calls=%fused_computation.19 | convolution fusion | flops 17237120 | bytes 1314816 | tf_op jit(solution)/shard_map/while/body/eval_jaxpr/while/body/eval_jaxpr/hqk,khd->qhd/dot_general | solution.py:38
  7.4 0.0 copy-done.1
  7.4 0.3 fusion.12
  7.6 15.1 %all_to_all.8 = bf16[1,16,8,512]{3,2,0,1:T(8,128)(2,1)S(1)} all-to-all(bf16[1,16,8,512]{3,2,0,1:T(8,128)(2,1)S(1)} %fusion.12), channel_id=1, replica_groups=mesh['groups'=2,'seq'=16] {'seq'}, dimensions={1} | all-to-all | bytes 262144 | tf_op jit(solution)/shard_map/all_to_all | solution.py:90
  22.8 0.1 convert_reduce_fusion.1
  22.9 0.1 div.53
  23.0 0.2 fusion.38
  23.2 0.1 rsqrt.33
  23.2 1.8 %convolution_convert_fusion = bf16[128,1536]{1,0:T(8,128)(2,1)S(1)} fusion(bf16[512,1536]{1,0:T(8,128)(2,1)} %param.10, bf16[1,16,8,512]{3,2,0,1:T(8,128)(2,1)S(1)} %all_to_all.8, f32[128]{0:T(128)S(1)} %rsqrt.33, f32[128]{0:T(128)S(1)} %div.53), kind=kOutput, calls=%fused_computation.2 | convolution fusion | flops 201785344 | bytes 2098176 | tf_op jit(solution)/shard_map/dot_general | solution.py:54
  25.1 0.4 %reshape.151 = bf16[16,8,3,8,64]{4,3,2,1,0:T(8,128)(2,1)S(1)} reshape(bf16[128,1536]{1,0:T(8,128)(2,1)S(1)} %convolution_convert_fusion) | data formatting | bytes 786432 | tf_op jit(solution)/shard_map/reshape | solution.py:57
  25.5 0.9 %fusion.66 = (bf16[16,8,1,8,64]{4,3,2,1,0:T(8,128)(2,1)S(1)}, bf16[16,8,1,8,64]{4,3,2,1,0:T(8,128)(2,1)}, bf16[16,8,1,8,64]{4,3,2,1,0:T(8,128)(2,1)S(1)}) fusion(bf16[16,8,3,8,64]{4,3,2,1,0:T(8,128)(2,1)S(1)} %reshape.151), kind=kLoop, calls=%fused_computation.88 | loop fusion | bytes 786432 | tf_op jit(solution)/shard_map/slice | solution.py:59
  26.5 1.1 %fusion.68 = f32[8,8,16]{2,1,0:T(8,128)} fusion(bf16[16,8,1,8,64]{4,3,2,1,0:T(8,128)(2,1)S(1)} %get-tuple-element.40, bf16[16,8,1,8,64]{4,3,2,1,0:T(8,128)(2,1)S(1)} %get-tuple-element.33), kind=kOutput, calls=%fused_computation.90 | convolution fusion | flops 2146319 | bytes 266240 | tf_op jit(solution)/shard_map/sub | solution.py:17
  27.6 0.4 convolution_multiply_fusion.1
  28.0 1.4 %fusion.6 = bf16[16,8,8,64]{3,0,2,1:T(8,128)(2,1)S(1)} fusion(bf16[16,8,1,8,64]{4,3,2,1,0:T(8,128)(2,1)} %get-tuple-element.34, f32[8,8,16]{2,1,0:T(8,128)} %fusion.68, f32[8,8,16,16]{2,3,1,0:T(8,128)S(1)} %convolution_multiply_fusion.1), kind=kOutput, calls=%fused_computation.12 | convolution fusion | flops 2212879 | bytes 331776 | tf_op jit(solution)/shard_map/khfg,gkhd->fkhd/dot_general | solution.py:62
  29.4 0.1 copy.30
  29.5 0.2 reshape.152
  29.7 0.2 fusion.11
  30.0 10.5 %all_to_all.9 = bf16[16,1,8,512]{3,2,1,0:T(8,128)(2,1)S(1)} all-to-all(bf16[16,1,8,512]{3,2,1,0:T(8,128)(2,1)S(1)} %fusion.11), channel_id=1, replica_groups=mesh['groups'=2,'seq'=16] {'seq'}, dimensions={0} | all-to-all | bytes 262144 | tf_op jit(solution)/shard_map/all_to_all | solution.py:96
  40.5 0.1 convert_reduce_fusion
  40.6 0.1 div.58
  40.7 0.2 fusion.40
  40.9 0.1 rsqrt.35
  41.0 3.2 %fusion.10 = bf16[1,128,512]{2,1,0:T(8,128)(2,1)} fusion(bf16[2048,512]{1,0:T(8,128)(2,1)S(1)} %copy-done, bf16[16,1,8,512]{3,2,1,0:T(8,128)(2,1)S(1)} %all_to_all.9, bf16[512,2048]{1,0:T(8,128)(2,1)} %param.12, f32[128]{0:T(128)S(1)} %rsqrt.35, f32[128]{0:T(128)S(1)} %div.58), kind=kOutput, calls=%fused_computation.20 | convolution fusion | flops 539688960 | bytes 4457472 | tf_op jit(solution)/shard_map/dot_general | solution.py:77
  (10 shorter events, 0.0 us)
Async XLA Ops:
  0.0 41.0 %copy-start = (bf16[2048,512]{1,0:T(8,128)(2,1)S(1)}, bf16[2048,512]{1,0:T(8,128)(2,1)}, u32[]{:S(2)}) copy-start(bf16[2048,512]{1,0:T(8,128)(2,1)} %param.13) | copy-start | bytes 6291460
  4.4 3.0 %copy-start.1 = (bf16[1,128,512]{2,1,0:T(8,128)(2,1)S(1)}, bf16[1,128,512]{2,1,0:T(8,128)(2,1)}, u32[]{:S(2)}) copy-start(bf16[1,128,512]{2,1,0:T(8,128)(2,1)} %param.7) | copy-start | bytes 393220
  4.4 3.0 %copy-start.2 = (bf16[512,512]{1,0:T(8,128)(2,1)S(1)}, bf16[512,512]{1,0:T(8,128)(2,1)}, u32[]{:S(2)}) copy-start(bf16[512,512]{1,0:T(8,128)(2,1)} %param.9) | copy-start | bytes 1572868
  28.0 1.7 %copy-start.3 = (bf16[512,512]{1,0:T(8,128)(2,1)S(1)}, bf16[512,512]{1,0:T(8,128)(2,1)}, u32[]{:S(2)}) copy-start(bf16[512,512]{1,0:T(8,128)(2,1)} %param.11) | copy-start | bytes 1572868
where the time goes:
time: 44.5 us; the launch traced here: 44.1 us
  blocking collectives  25.6 us (58%)
  matrix products  13.3 us (30%)
  other arithmetic  2.81 us (6%)
  local copies, waits for them, and re-layouts  2.23 us (5%)
    all_to_all x1, blocking collectives, local(): lax.all_to_all(blocks, 'seq', split_axis=1, concat_axis=0, tiled=True)  15.1 us
    all_to_all x1, blocking collectives, local(): lax.all_to_all(returned, 'seq', split_axis=0, concat_axis=1, tiled=True)  10.5 us
    dot_general x1, matrix products, feed_forward(): jnp.dot(hidden, w_down, preferred_element_type=jnp.float32)  3.19 us
    dot_general x1, matrix products, spatial_frame(): jnp.dot(norm_rows(frame_rows.astype(jnp.float32)), w_qkv, preferred_eleme...  1.9 us
    dot_general x1, matrix products, temporal_block(): jnp.dot(norm_rows(flat_rows.astype(jnp.float32)), w_qkv, preferred_elemen...  1.82 us
    sub x2, matrix products, softmax_rows(): raised = jnp.exp(scores - row_max)  1.51 us
    dot_general x1, matrix products, one_block(): jnp.einsum('hqk,khd->qhd', weights, value_rows, preferred_element_type=jn...  1.47 us
    reduce_sum x3, other arithmetic, norm_rows(): spread = jnp.mean(center * center, axis=-1, keepdims=True)  1.43 us

commit v1 on v0

--- a/solution.py
+++ b/solution.py
@@ -4,6 +4,22 @@
 from jax.sharding import PartitionSpec as P
 
 HEADS = 8
+
+
+def exchange_in_pairs(value, axis, split, join):
+    ways, here = (lax.axis_size(axis), lax.axis_index(axis))
+    width = value.shape[split] // ways
+    dims = list(value.shape)
+    dims[split] = width
+    height = dims[join]
+    dims[join] = height * ways
+    full = jnp.zeros(dims, value.dtype)
+    for mask in range(ways):
+        part = lax.dynamic_slice_in_dim(value, (here ^ mask) * width, width, axis=split)
+        if mask:
+            part = lax.ppermute(part, axis, [(d, d ^ mask) for d in range(ways)])
+        full = lax.dynamic_update_slice_in_dim(full, part, (here ^ mask) * height, axis=join)
+    return full
 
 
 def norm_rows(values):
@@ -93,7 +109,7 @@
     tokens = arrived.reshape(frames, count_rows, model_width)
     after_time = temporal_block(tokens, temporal_qkv, temporal_out)
     returned = after_time.reshape(frames, 1, count_rows, model_width)
-    arrived_back = lax.all_to_all(returned, "seq", split_axis=0, concat_axis=1, tiled=True)
+    arrived_back = exchange_in_pairs(returned, "seq", 0, 1)
     result_rows = arrived_back.reshape(frame_count * patches, model_width)
     result_rows = feed_forward(result_rows, mlp_up, mlp_down)
     return result_rows.reshape(frame_count, patches, model_width)

time: 44.5 us -> 58 us (1.30)
  starting transfers between devices: 0 us -> 28 us
  blocking collectives: 25.6 us -> 0 us
  waiting for transfers between devices: 0 us -> 10.2 us
  matrix products: 13.3 us -> 13.9 us
    all_to_all x2 -> x0, blocking collectives: 25.6 us -> none  [the longest x1 15.1 us: local(): lax.all_to_all(blocks, 'seq', split_axis=1, concat_axis=0, tiled=True)]
    ppermute x0 -> x15, starting transfers between devices: none -> 20.5 us  [exchange_in_pairs(): part = lax.ppermute(part, axis, [(d, d ^ mask) for d in range(ways)])]
    all_to_all x0 -> x1, waiting for transfers between devices: none -> 7.82 us  [local(): lax.all_to_all(blocks, 'seq', split_axis=1, concat_axis=0, tiled=True)]
    all_to_all x0 -> x1, starting transfers between devices: none -> 7.41 us  [local(): lax.all_to_all(blocks, 'seq', split_axis=1, concat_axis=0, tiled=True)]
    ppermute x0 -> x15, waiting for transfers between devices: none -> 2.38 us  [exchange_in_pairs(): part = lax.ppermute(part, axis, [(d, d ^ mask) for d in range(ways)])]
    dot_general x1, matrix products: 0.25 us -> 0.91 us  [spatial_frame(): jnp.dot(attended, w_out, preferred_element_type=jnp.float32)]
  transfers between devices with their start and end apart: 0 -> 16, of which waited for: 0 -> 3; matrix products, arithmetic and copies ran while one was open for 0% -> 0% of each run, Pallas kernels for 0% -> 0%
where the time goes in v1:
time: 58 us; the launch traced here: 57.7 us
  starting transfers between devices  28 us (48%)
  matrix products  13.9 us (24%)
  waiting for transfers between devices  10.2 us (18%)
  other arithmetic  2.81 us (5%)
  local copies, waits for them, and re-layouts  2.37 us (4%)
    ppermute x15, starting transfers between devices, exchange_in_pairs(): part = lax.ppermute(part, axis, [(d, d ^ mask) for d in range(ways)])  20.5 us
    all_to_all x1, waiting for transfers between devices, local(): lax.all_to_all(blocks, 'seq', split_axis=1, concat_axis=0, tiled=True)  7.82 us
    all_to_all x1, starting transfers between devices, local(): lax.all_to_all(blocks, 'seq', split_axis=1, concat_axis=0, tiled=True)  7.41 us
    dot_general x1, matrix products, feed_forward(): jnp.dot(hidden, w_down, preferred_element_type=jnp.float32)  3.19 us
    ppermute x15, waiting for transfers between devices, exchange_in_pairs(): part = lax.ppermute(part, axis, [(d, d ^ mask) for d in range(ways)])  2.38 us
    dot_general x1, matrix products, spatial_frame(): jnp.dot(norm_rows(frame_rows.astype(jnp.float32)), w_qkv, preferred_eleme...  1.9 us
    dot_general x1, matrix products, temporal_block(): jnp.dot(norm_rows(flat_rows.astype(jnp.float32)), w_qkv, preferred_elemen...  1.83 us
    sub x2, matrix products, softmax_rows(): raised = jnp.exp(scores - row_max)  1.52 us
  transfers between devices with their start and end apart: 16, of which 3 were waited for; matrix products, arithmetic and copies ran while one was open for 0% of the time, Pallas kernels for 0%

profile of v1, /device:TPU:0, one launch (start us, length us, event | category | flops | bytes accessed | tf_op | source)
XLA Modules:
  0.0 57.7 jit_solution(13901902067970848285)
XLA Ops:
  0.0 1.2 %convert_reduce_fusion.2 = f32[128]{0:T(128)S(1)} fusion(bf16[1,128,512]{2,1,0:T(8,128)(2,1)} %param.7), kind=kLoop, calls=%fused_computation.45 | loop fusion | flops 130944 | bytes 131584 | tf_op jit(solution)/shard_map/while/body/eval_jaxpr/reduce_sum | solution.py:26
  1.2 1.1 %fusion.31 = f32[128]{0:T(128)S(1)} fusion(bf16[1,128,512]{2,1,0:T(8,128)(2,1)} %param.7, f32[128]{0:T(128)S(1)} %broadcast_multiply_fusion.2), kind=kLoop, calls=%fused_computation.50 | loop fusion | flops 262016 | bytes 132096 | tf_op jit(solution)/shard_map/while/body/eval_jaxpr/reduce_sum | solution.py:27
  2.3 1.9 %convolution_convert_fusion.1 = bf16[128,1536]{1,0:T(8,128)(2,1)S(1)} fusion(bf16[512,1536]{1,0:T(8,128)(2,1)} %param.8, bf16[1,128,512]{2,1,0:T(8,128)(2,1)} %param.7, f32[128]{0:T(128)S(1)} %add_rsqrt_fusion.2, f32[128]{0:T(128)S(1)} %broadcast_multiply_fusion.2), kind=kOutput, calls=%fused_computation.3 | convolution fusion | flops 201785344 | bytes 2098176 | tf_op jit(solution)/shard_map/while/body/eval_jaxpr/dot_general | solution.py:40
  4.2 0.2 copy.55
  4.4 1.1 %convolution_multiply_fusion = f32[8,128,128]{1,2,0:T(8,128)} fusion(bf16[128,3,8,64]{0,3,2,1:T(8,128)(2,1)S(1)} %bitcast.133), kind=kOutput, calls=%fused_computation.9 | convolution fusion | flops 16908288 | bytes 786432 | tf_op jit(solution)/shard_map/while/body/eval_jaxpr/while/body/eval_jaxpr/qhd,khd->hqk/dot_general | solution.py:50
  5.5 0.4 fusion.67
  5.9 1.5 %convolution_convert_fusion.3 = bf16[8,64,128]{2,1,0:T(8,128)(2,1)S(1)} fusion(f32[8,128]{1,0:T(8,128)S(1)} %fusion.67, bf16[128,3,8,64]{0,3,2,1:T(8,128)(2,1)S(1)} %bitcast.135, f32[8,128,128]{1,2,0:T(8,128)} %convolution_multiply_fusion), kind=kOutput, calls=%fused_computation.19 | convolution fusion | flops 17237120 | bytes 1314816 | tf_op jit(solution)/shard_map/while/body/eval_jaxpr/while/body/eval_jaxpr/hqk,khd->qhd/dot_general | solution.py:54
  7.4 0.9 %fusion.12 = bf16[1,16,8,512]{3,2,0,1:T(8,128)(2,1)} fusion(bf16[128,512]{0,1:T(8,128)(2,1)S(1)} %bitcast.136, bf16[512,512]{1,0:T(8,128)(2,1)S(1)} %copy-done.2, bf16[1,128,512]{2,1,0:T(8,128)(2,1)S(1)} %copy-done.1), kind=kOutput, calls=%fused_computation.22 | convolution fusion | flops 67305472 | bytes 917504 | tf_op jit(solution)/shard_map/while/body/eval_jaxpr/dot_general | solution.py:60
  8.3 7.4 %all-to-all-start = ((bf16[1,16,8,512]{3,2,0,1:T(8,128)(2,1)}), bf16[1,16,8,512]{3,2,0,1:T(8,128)(2,1)S(1)}, u32[]{:S(2)}, u32[]{:S(2)}) async-start(bf16[1,16,8,512]{3,2,0,1:T(8,128)(2,1)} %fusion.12), calls=%async_computation | async-start | bytes 262144 | tf_op jit(solution)/shard_map/all_to_all | solution.py:106
  15.8 7.8 %all-to-all-done = bf16[1,16,8,512]{3,2,0,1:T(8,128)(2,1)S(1)} async-done(((bf16[1,16,8,512]{3,2,0,1:T(8,128)(2,1)}), bf16[1,16,8,512]{3,2,0,1:T(8,128)(2,1)S(1)}, u32[]{:S(2)}, u32[]{:S(2)}) %all-to-all-start) | async-done | bytes 131104 | tf_op jit(solution)/shard_map/all_to_all | solution.py:106
  24.1 1.8 %convolution_convert_fusion = bf16[128,1536]{1,0:T(8,128)(2,1)S(1)} fusion(bf16[512,1536]{1,0:T(8,128)(2,1)} %param.10, bf16[1,16,8,512]{3,2,0,1:T(8,128)(2,1)S(1)} %all-to-all-done, f32[128]{0:T(128)S(1)} %rsqrt.33, f32[128]{0:T(128)S(1)} %div.53), kind=kOutput, calls=%fused_computation.2 | convolution fusion | flops 201785344 | bytes 2098176 | tf_op jit(solution)/shard_map/dot_general | solution.py:70
  25.9 0.4 reshape.137
  26.4 0.9 %fusion.66 = (bf16[16,8,1,8,64]{4,3,2,1,0:T(8,128)(2,1)S(1)}, bf16[16,8,1,8,64]{4,3,2,1,0:T(8,128)(2,1)}, bf16[16,8,1,8,64]{4,3,2,1,0:T(8,128)(2,1)S(1)}) fusion(bf16[16,8,3,8,64]{4,3,2,1,0:T(8,128)(2,1)S(1)} %reshape.137), kind=kLoop, calls=%fused_computation.119 | loop fusion | bytes 786432 | tf_op jit(solution)/shard_map/slice | solution.py:75
  27.3 0.4 convolution_multiply_fusion.1
  27.7 1.2 %fusion.68 = f32[8,8,16]{2,1,0:T(8,128)} fusion(bf16[16,8,1,8,64]{4,3,2,1,0:T(8,128)(2,1)S(1)} %get-tuple-element.40, bf16[16,8,1,8,64]{4,3,2,1,0:T(8,128)(2,1)S(1)} %get-tuple-element.33), kind=kOutput, calls=%fused_computation.121 | convolution fusion | flops 2146319 | bytes 266240 | tf_op jit(solution)/shard_map/sub | solution.py:33
  28.9 1.4 %fusion.6 = bf16[16,8,8,64]{3,0,2,1:T(8,128)(2,1)S(1)} fusion(bf16[16,8,1,8,64]{4,3,2,1,0:T(8,128)(2,1)} %get-tuple-element.34, f32[8,8,16]{2,1,0:T(8,128)} %fusion.68, f32[8,8,16,16]{2,3,1,0:T(8,128)S(1)} %convolution_multiply_fusion.1), kind=kOutput, calls=%fused_computation.12 | convolution fusion | flops 2212879 | bytes 331776 | tf_op jit(solution)/shard_map/khfg,gkhd->fkhd/dot_general | solution.py:78
  30.4 0.2 reshape.138
  30.6 0.2 fusion.11
  31.1 1.8 %collective-permute-start.2 = (bf16[1,1,8,512]{3,2,0,1:T(8,128)(2,1)S(1)}, bf16[1,1,8,512]{3,2,0,1:T(8,128)(2,1)S(1)}, u32[]{:S(2)}, u32[]{:S(2)}) collective-permute-start(bf16[1,1,8,512]{3,2,0,1:T(8,128)(2,1)S(1)} %get-tuple-element.55), channel_id=1, source_target_pairs={{0,3},{1,2},{2,1},{3,0},{4,7},{5,6},{6,5},{7,4},{8,11},{9,10},{10,... | collective-permute-start | bytes 24584 | tf_op jit(solution)/shard_map/ppermute | solution.py:20
  32.9 1.7 %collective-permute-start.4 = (bf16[1,1,8,512]{3,2,0,1:T(8,128)(2,1)S(1)}, bf16[1,1,8,512]{3,2,0,1:T(8,128)(2,1)S(1)}, u32[]{:S(2)}, u32[]{:S(2)}) collective-permute-start(bf16[1,1,8,512]{3,2,0,1:T(8,128)(2,1)S(1)} %get-tuple-element.53), channel_id=1, source_target_pairs={{0,5},{1,4},{2,7},{3,6},{4,1},{5,0},{6,3},{7,2},{8,13},{9,12},{10,... | collective-permute-start | bytes 24584 | tf_op jit(solution)/shard_map/ppermute | solution.py:20
  34.8 2.6 %collective-permute-start.6 = (bf16[1,1,8,512]{3,2,0,1:T(8,128)(2,1)S(1)}, bf16[1,1,8,512]{3,2,0,1:T(8,128)(2,1)S(1)}, u32[]{:S(2)}, u32[]{:S(2)}) collective-permute-start(bf16[1,1,8,512]{3,2,0,1:T(8,128)(2,1)S(1)} %get-tuple-element.51), channel_id=1, source_target_pairs={{0,7},{1,6},{2,5},{3,4},{4,3},{5,2},{6,1},{7,0},{8,15},{9,14},{10,... | collective-permute-start | bytes 24584 | tf_op jit(solution)/shard_map/ppermute | solution.py:20
  37.4 0.4 collective-permute-start.7
  37.8 2.2 %collective-permute-start.8 = (bf16[1,1,8,512]{3,2,0,1:T(8,128)(2,1)S(1)}, bf16[1,1,8,512]{3,2,0,1:T(8,128)(2,1)S(1)}, u32[]{:S(2)}, u32[]{:S(2)}) collective-permute-start(bf16[1,1,8,512]{3,2,0,1:T(8,128)(2,1)S(1)} %get-tuple-element.49), channel_id=1, source_target_pairs={{0,9},{1,8},{2,11},{3,10},{4,13},{5,12},{6,15},{7,14},{8,1},{9,0},... | collective-permute-start | bytes 24584 | tf_op jit(solution)/shard_map/ppermute | solution.py:20
  40.0 0.3 collective-permute-start.9
  40.3 3.3 %collective-permute-start.10 = (bf16[1,1,8,512]{3,2,0,1:T(8,128)(2,1)S(1)}, bf16[1,1,8,512]{3,2,0,1:T(8,128)(2,1)S(1)}, u32[]{:S(2)}, u32[]{:S(2)}) collective-permute-start(bf16[1,1,8,512]{3,2,0,1:T(8,128)(2,1)S(1)} %get-tuple-element.47), channel_id=1, source_target_pairs={{0,11},{1,10},{2,9},{3,8},{4,15},{5,14},{6,13},{7,12},{8,3},{9,2},... | collective-permute-start | bytes 24584 | tf_op jit(solution)/shard_map/ppermute | solution.py:20
  43.6 0.7 %collective-permute-start.11 = (bf16[1,1,8,512]{3,2,0,1:T(8,128)(2,1)S(1)}, bf16[1,1,8,512]{3,2,0,1:T(8,128)(2,1)S(1)}, u32[]{:S(2)}, u32[]{:S(2)}) collective-permute-start(bf16[1,1,8,512]{3,2,0,1:T(8,128)(2,1)S(1)} %get-tuple-element.46), channel_id=1, source_target_pairs={{0,12},{1,13},{2,14},{3,15},{4,8},{5,9},{6,10},{7,11},{8,4},{9,5},... | collective-permute-start | bytes 24584 | tf_op jit(solution)/shard_map/ppermute | solution.py:20
  44.3 2.8 %collective-permute-start.12 = (bf16[1,1,8,512]{3,2,0,1:T(8,128)(2,1)S(1)}, bf16[1,1,8,512]{3,2,0,1:T(8,128)(2,1)S(1)}, u32[]{:S(2)}, u32[]{:S(2)}) collective-permute-start(bf16[1,1,8,512]{3,2,0,1:T(8,128)(2,1)S(1)} %get-tuple-element.45), channel_id=1, source_target_pairs={{0,13},{1,12},{2,15},{3,14},{4,9},{5,8},{6,11},{7,10},{8,5},{9,4},... | collective-permute-start | bytes 24584 | tf_op jit(solution)/shard_map/ppermute | solution.py:20
  47.1 1.1 %collective-permute-start.13 = (bf16[1,1,8,512]{3,2,0,1:T(8,128)(2,1)S(1)}, bf16[1,1,8,512]{3,2,0,1:T(8,128)(2,1)S(1)}, u32[]{:S(2)}, u32[]{:S(2)}) collective-permute-start(bf16[1,1,8,512]{3,2,0,1:T(8,128)(2,1)S(1)} %get-tuple-element.44), channel_id=1, source_target_pairs={{0,14},{1,15},{2,12},{3,13},{4,10},{5,11},{6,8},{7,9},{8,6},{9,7},... | collective-permute-start | bytes 24584 | tf_op jit(solution)/shard_map/ppermute | solution.py:20
  48.2 3.4 %collective-permute-start.14 = (bf16[1,1,8,512]{3,2,0,1:T(8,128)(2,1)S(1)}, bf16[1,1,8,512]{3,2,0,1:T(8,128)(2,1)S(1)}, u32[]{:S(2)}, u32[]{:S(2)}) collective-permute-start(bf16[1,1,8,512]{3,2,0,1:T(8,128)(2,1)S(1)} %get-tuple-element.42), channel_id=1, source_target_pairs={{0,15},{1,14},{2,13},{3,12},{4,11},{5,10},{6,9},{7,8},{8,7},{9,6},... | collective-permute-start | bytes 24584 | tf_op jit(solution)/shard_map/ppermute | solution.py:20
  51.6 1.8 %collective-permute-done.13 = bf16[1,1,8,512]{3,2,0,1:T(8,128)(2,1)S(1)} collective-permute-done((bf16[1,1,8,512]{3,2,0,1:T(8,128)(2,1)S(1)}, bf16[1,1,8,512]{3,2,0,1:T(8,128)(2,1)S(1)}, u32[]{:S(2)}, u32[]{:S(2)}) %collective-permute-start.13) | collective-permute-done | bytes 8224 | tf_op jit(solution)/shard_map/ppermute | solution.py:20
  53.4 0.5 collective-permute-done.14
  54.5 3.2 %fusion.10 = bf16[1,128,512]{2,1,0:T(8,128)(2,1)} fusion(bf16[2048,512]{1,0:T(8,128)(2,1)S(1)} %copy-done, bf16[1,16,8,512]{3,2,1,0:T(8,128)(2,1)S(1)} %bitcast_dynamic-update-slice_fusion, bf16[512,2048]{1,0:T(8,128)(2,1)} %param.12, f32[128]{0:T(128)S(1)} %rsqrt.35, f32[128]{0:T(128)S(1)} %div.58), kind=kOutput, calls=%fused_computation.20 | convolution fusion | flops 539688960 | bytes 4457472 | tf_op jit(solution)/shard_map/dot_general | solution.py:93
  (58 shorter events, 1.5 us)
Async XLA Ops:
  0.0 54.5 %copy-start = (bf16[2048,512]{1,0:T(8,128)(2,1)S(1)}, bf16[2048,512]{1,0:T(8,128)(2,1)}, u32[]{:S(2)}) copy-start(bf16[2048,512]{1,0:T(8,128)(2,1)} %param.13) | copy-start | bytes 6291460
  4.4 3.0 %copy-start.1 = (bf16[1,128,512]{2,1,0:T(8,128)(2,1)S(1)}, bf16[1,128,512]{2,1,0:T(8,128)(2,1)}, u32[]{:S(2)}) copy-start(bf16[1,128,512]{2,1,0:T(8,128)(2,1)} %param.7) | copy-start | bytes 393220
  4.4 3.0 %copy-start.2 = (bf16[512,512]{1,0:T(8,128)(2,1)S(1)}, bf16[512,512]{1,0:T(8,128)(2,1)}, u32[]{:S(2)}) copy-start(bf16[512,512]{1,0:T(8,128)(2,1)} %param.9) | copy-start | bytes 1572868
  8.3 15.3 %all-to-all-start = ((bf16[1,16,8,512]{3,2,0,1:T(8,128)(2,1)}), bf16[1,16,8,512]{3,2,0,1:T(8,128)(2,1)S(1)}, u32[]{:S(2)}, u32[]{:S(2)}) async-start(bf16[1,16,8,512]{3,2,0,1:T(8,128)(2,1)} %fusion.12), calls=%async_computation | async-start | bytes 262144 | tf_op jit(solution)/shard_map/all_to_all | solution.py:106
  28.9 1.7 %copy-start.3 = (bf16[512,512]{1,0:T(8,128)(2,1)S(1)}, bf16[512,512]{1,0:T(8,128)(2,1)}, u32[]{:S(2)}) copy-start(bf16[512,512]{1,0:T(8,128)(2,1)} %param.11) | copy-start | bytes 1572868
  30.9 3.7 %collective-permute-start = (bf16[1,1,8,512]{3,2,0,1:T(8,128)(2,1)S(1)}, bf16[1,1,8,512]{3,2,0,1:T(8,128)(2,1)S(1)}, u32[]{:S(2)}, u32[]{:S(2)}) collective-permute-start(bf16[1,1,8,512]{3,2,0,1:T(8,128)(2,1)S(1)} %get-tuple-element.57), channel_id=1, source_target_pairs={{0,1},{1,0},{2,3},{3,2},{4,5},{5,4},{6,7},{7,6},{8,9},{9,8},{10,11... | collective-permute-start | bytes 24584 | tf_op jit(solution)/shard_map/ppermute | solution.py:20
  31.0 3.8 %collective-permute-start.1 = (bf16[1,1,8,512]{3,2,0,1:T(8,128)(2,1)S(1)}, bf16[1,1,8,512]{3,2,0,1:T(8,128)(2,1)S(1)}, u32[]{:S(2)}, u32[]{:S(2)}) collective-permute-start(bf16[1,1,8,512]{3,2,0,1:T(8,128)(2,1)S(1)} %get-tuple-element.56), channel_id=1, source_target_pairs={{0,2},{1,3},{2,0},{3,1},{4,6},{5,7},{6,4},{7,5},{8,10},{9,11},{10,... | collective-permute-start | bytes 24584 | tf_op jit(solution)/shard_map/ppermute | solution.py:20
  31.1 6.3 %collective-permute-start.2 = (bf16[1,1,8,512]{3,2,0,1:T(8,128)(2,1)S(1)}, bf16[1,1,8,512]{3,2,0,1:T(8,128)(2,1)S(1)}, u32[]{:S(2)}, u32[]{:S(2)}) collective-permute-start(bf16[1,1,8,512]{3,2,0,1:T(8,128)(2,1)S(1)} %get-tuple-element.55), channel_id=1, source_target_pairs={{0,3},{1,2},{2,1},{3,0},{4,7},{5,6},{6,5},{7,4},{8,11},{9,10},{10,... | collective-permute-start | bytes 24584 | tf_op jit(solution)/shard_map/ppermute | solution.py:20
  32.8 4.9 %collective-permute-start.3 = (bf16[1,1,8,512]{3,2,0,1:T(8,128)(2,1)S(1)}, bf16[1,1,8,512]{3,2,0,1:T(8,128)(2,1)S(1)}, u32[]{:S(2)}, u32[]{:S(2)}) collective-permute-start(bf16[1,1,8,512]{3,2,0,1:T(8,128)(2,1)S(1)} %get-tuple-element.54), channel_id=1, source_target_pairs={{0,4},{1,5},{2,6},{3,7},{4,0},{5,1},{6,2},{7,3},{8,12},{9,13},{10,... | collective-permute-start | bytes 24584 | tf_op jit(solution)/shard_map/ppermute | solution.py:20
  32.9 7.1 %collective-permute-start.4 = (bf16[1,1,8,512]{3,2,0,1:T(8,128)(2,1)S(1)}, bf16[1,1,8,512]{3,2,0,1:T(8,128)(2,1)S(1)}, u32[]{:S(2)}, u32[]{:S(2)}) collective-permute-start(bf16[1,1,8,512]{3,2,0,1:T(8,128)(2,1)S(1)} %get-tuple-element.53), channel_id=1, source_target_pairs={{0,5},{1,4},{2,7},{3,6},{4,1},{5,0},{6,3},{7,2},{8,13},{9,12},{10,... | collective-permute-start | bytes 24584 | tf_op jit(solution)/shard_map/ppermute | solution.py:20
  34.6 5.7 %collective-permute-start.5 = (bf16[1,1,8,512]{3,2,0,1:T(8,128)(2,1)S(1)}, bf16[1,1,8,512]{3,2,0,1:T(8,128)(2,1)S(1)}, u32[]{:S(2)}, u32[]{:S(2)}) collective-permute-start(bf16[1,1,8,512]{3,2,0,1:T(8,128)(2,1)S(1)} %get-tuple-element.52), channel_id=1, source_target_pairs={{0,6},{1,7},{2,4},{3,5},{4,2},{5,3},{6,0},{7,1},{8,14},{9,15},{10,... | collective-permute-start | bytes 24584 | tf_op jit(solution)/shard_map/ppermute | solution.py:20
  34.8 8.8 %collective-permute-start.6 = (bf16[1,1,8,512]{3,2,0,1:T(8,128)(2,1)S(1)}, bf16[1,1,8,512]{3,2,0,1:T(8,128)(2,1)S(1)}, u32[]{:S(2)}, u32[]{:S(2)}) collective-permute-start(bf16[1,1,8,512]{3,2,0,1:T(8,128)(2,1)S(1)} %get-tuple-element.51), channel_id=1, source_target_pairs={{0,7},{1,6},{2,5},{3,4},{4,3},{5,2},{6,1},{7,0},{8,15},{9,14},{10,... | collective-permute-start | bytes 24584 | tf_op jit(solution)/shard_map/ppermute | solution.py:20
  37.4 6.9 %collective-permute-start.7 = (bf16[1,1,8,512]{3,2,0,1:T(8,128)(2,1)S(1)}, bf16[1,1,8,512]{3,2,0,1:T(8,128)(2,1)S(1)}, u32[]{:S(2)}, u32[]{:S(2)}) collective-permute-start(bf16[1,1,8,512]{3,2,0,1:T(8,128)(2,1)S(1)} %get-tuple-element.50), channel_id=1, source_target_pairs={{0,8},{1,9},{2,10},{3,11},{4,12},{5,13},{6,14},{7,15},{8,0},{9,1},... | collective-permute-start | bytes 24584 | tf_op jit(solution)/shard_map/ppermute | solution.py:20
  37.8 9.3 %collective-permute-start.8 = (bf16[1,1,8,512]{3,2,0,1:T(8,128)(2,1)S(1)}, bf16[1,1,8,512]{3,2,0,1:T(8,128)(2,1)S(1)}, u32[]{:S(2)}, u32[]{:S(2)}) collective-permute-start(bf16[1,1,8,512]{3,2,0,1:T(8,128)(2,1)S(1)} %get-tuple-element.49), channel_id=1, source_target_pairs={{0,9},{1,8},{2,11},{3,10},{4,13},{5,12},{6,15},{7,14},{8,1},{9,0},... | collective-permute-start | bytes 24584 | tf_op jit(solution)/shard_map/ppermute | solution.py:20
  40.0 8.2 %collective-permute-start.9 = (bf16[1,1,8,512]{3,2,0,1:T(8,128)(2,1)S(1)}, bf16[1,1,8,512]{3,2,0,1:T(8,128)(2,1)S(1)}, u32[]{:S(2)}, u32[]{:S(2)}) collective-permute-start(bf16[1,1,8,512]{3,2,0,1:T(8,128)(2,1)S(1)} %get-tuple-element.48), channel_id=1, source_target_pairs={{0,10},{1,11},{2,8},{3,9},{4,14},{5,15},{6,12},{7,13},{8,2},{9,3},... | collective-permute-start | bytes 24584 | tf_op jit(solution)/shard_map/ppermute | solution.py:20
  40.3 11.3 %collective-permute-start.10 = (bf16[1,1,8,512]{3,2,0,1:T(8,128)(2,1)S(1)}, bf16[1,1,8,512]{3,2,0,1:T(8,128)(2,1)S(1)}, u32[]{:S(2)}, u32[]{:S(2)}) collective-permute-start(bf16[1,1,8,512]{3,2,0,1:T(8,128)(2,1)S(1)} %get-tuple-element.47), channel_id=1, source_target_pairs={{0,11},{1,10},{2,9},{3,8},{4,15},{5,14},{6,13},{7,12},{8,3},{9,2},... | collective-permute-start | bytes 24584 | tf_op jit(solution)/shard_map/ppermute | solution.py:20
  43.6 8.0 %collective-permute-start.11 = (bf16[1,1,8,512]{3,2,0,1:T(8,128)(2,1)S(1)}, bf16[1,1,8,512]{3,2,0,1:T(8,128)(2,1)S(1)}, u32[]{:S(2)}, u32[]{:S(2)}) collective-permute-start(bf16[1,1,8,512]{3,2,0,1:T(8,128)(2,1)S(1)} %get-tuple-element.46), channel_id=1, source_target_pairs={{0,12},{1,13},{2,14},{3,15},{4,8},{5,9},{6,10},{7,11},{8,4},{9,5},... | collective-permute-start | bytes 24584 | tf_op jit(solution)/shard_map/ppermute | solution.py:20
  44.3 7.4 %collective-permute-start.12 = (bf16[1,1,8,512]{3,2,0,1:T(8,128)(2,1)S(1)}, bf16[1,1,8,512]{3,2,0,1:T(8,128)(2,1)S(1)}, u32[]{:S(2)}, u32[]{:S(2)}) collective-permute-start(bf16[1,1,8,512]{3,2,0,1:T(8,128)(2,1)S(1)} %get-tuple-element.45), channel_id=1, source_target_pairs={{0,13},{1,12},{2,15},{3,14},{4,9},{5,8},{6,11},{7,10},{8,5},{9,4},... | collective-permute-start | bytes 24584 | tf_op jit(solution)/shard_map/ppermute | solution.py:20
  47.1 6.3 %collective-permute-start.13 = (bf16[1,1,8,512]{3,2,0,1:T(8,128)(2,1)S(1)}, bf16[1,1,8,512]{3,2,0,1:T(8,128)(2,1)S(1)}, u32[]{:S(2)}, u32[]{:S(2)}) collective-permute-start(bf16[1,1,8,512]{3,2,0,1:T(8,128)(2,1)S(1)} %get-tuple-element.44), channel_id=1, source_target_pairs={{0,14},{1,15},{2,12},{3,13},{4,10},{5,11},{6,8},{7,9},{8,6},{9,7},... | collective-permute-start | bytes 24584 | tf_op jit(solution)/shard_map/ppermute | solution.py:20
  48.2 5.8 %collective-permute-start.14 = (bf16[1,1,8,512]{3,2,0,1:T(8,128)(2,1)S(1)}, bf16[1,1,8,512]{3,2,0,1:T(8,128)(2,1)S(1)}, u32[]{:S(2)}, u32[]{:S(2)}) collective-permute-start(bf16[1,1,8,512]{3,2,0,1:T(8,128)(2,1)S(1)} %get-tuple-element.42), channel_id=1, source_target_pairs={{0,15},{1,14},{2,13},{3,12},{4,11},{5,10},{6,9},{7,8},{8,7},{9,6},... | collective-permute-start | bytes 24584 | tf_op jit(solution)/shard_map/ppermute | solution.py:20
